TPU v7x, 256 devices: a whole 4x4x8 slice. The times are simulated.
256 devices in a mesh: ex: 2 (over core), slab: 128 (over z, y, x).
Axes of the slice: x: 4, y: 4, z: 8, core: 2. Of those that a mesh axis runs over, the one named last changes fastest.
Arguments:
- volume: bfloat16 [2, 16, 128, 32, 128], P('ex', None, 'slab'), may hold values from -6 to 6
- cotangent: bfloat16 [2, 16, 128, 32, 128], P('ex', None, 'slab')
- gate_mask: int32 [2, 2, 128, 32, 128], P('ex', None, 'slab'), may hold values 0 or 1
- loss_scale: float32 [2], P('ex'), may hold values from 0.05 to 5
- canary: int32 [2], P('ex'), may hold values from 0 to 15
- kernels: bfloat16 [2, 32, 432], replicated, may hold values from -0.3125 to 0.3125
Outputs:
- input_grad: float32 [2, 16, 128, 32, 128], P('ex', None, 'slab')
- kernel_grad: float32 [2, 32, 432], replicated
All inputs are finite; a program needn't handle non-finite values. No bound on the sum of `gate_mask` on one device may be relied on, other than what follows from the above.
Results may differ from a plain program's by a relative error of at most 0.0037.
Values may be sent and summed in bfloat16 or wider, within the bound.
A program may use at most 64 MiB of HBM per device.

v0:
```python
import jax
import jax.numpy as jnp
from jax import lax
from jax.sharding import PartitionSpec as P


def with_halo(array, sides, width):
    for axis, dim in sides:
        peers, length = (lax.axis_size(axis), array.shape[dim])
        up = [(i, (i + 1) % peers) for i in range(peers - 1)]
        down = [(j, i) for i, j in up]
        last = lax.slice_in_dim(array, length - width, length, axis=dim)
        leading = lax.slice_in_dim(array, 0, width, axis=dim)
        before = lax.ppermute(last, axis, up)
        after = lax.ppermute(leading, axis, down)
        array = jnp.concatenate([before, array, after], axis=dim)
    return array


def columns(extended):
    zs = extended.shape[2] - 2
    hs, ws = (extended.shape[3], extended.shape[4])
    padded = jnp.pad(extended, ((0, 0), (0, 0), (0, 0), (1, 1), (1, 1)))
    taps = []
    for dz in range(3):
        for dh in range(3):
            for dw in range(3):
                taps.append(padded[:, :, dz : dz + zs, dh : dh + hs, dw : dw + ws])
    stacked = jnp.stack(taps, axis=1)
    return stacked.reshape((extended.shape[0], 27 * extended.shape[1], zs, hs, ws))


def back_columns(extended):
    zs = extended.shape[2] - 2
    hs, ws = (extended.shape[3], extended.shape[4])
    padded = jnp.pad(extended, ((0, 0), (0, 0), (0, 0), (1, 1), (1, 1)))
    taps = []
    for dz in range(3):
        for dh in range(3):
            for dw in range(3):
                taps.append(
                    padded[:, :, 2 - dz : 2 - dz + zs, 2 - dh : 2 - dh + hs, 2 - dw : 2 - dw + ws]
                )
    return jnp.stack(taps, axis=1)


def layer_forward(field, kernel):
    extended = with_halo(field, (("slab", 2),), 1)
    patches = columns(extended)
    pre = jnp.einsum("ok,ekzhw->eozhw", kernel, patches, preferred_element_type=jnp.float32)
    return (pre, patches)


def layer_backward(delta, kernel, patches):
    grads = jnp.einsum("eozhw,ekzhw->eok", delta, patches, preferred_element_type=jnp.float32)
    extended = with_halo(delta, (("slab", 2),), 1)
    width = kernel.shape[1] // 27
    shaped = kernel.reshape((kernel.shape[0], 27, width))
    spread = jnp.einsum(
        "otc,etozhw->eczhw", shaped, back_columns(extended), preferred_element_type=jnp.float32
    )
    return (grads, spread)


def per_device(volume, cotangent, gate_mask, loss_scale, canary, kernels):
    chans = volume.shape[1]
    local_ex = volume.shape[0]
    mask_one = gate_mask[:, 0][:, None].astype(jnp.float32)
    mask_two = gate_mask[:, 1][:, None].astype(jnp.float32)
    pre_one, patches_one = layer_forward(volume, kernels[0])
    value_one = pre_one[:, :chans]
    sig_one = jax.nn.sigmoid(pre_one[:, chans:])
    hidden = (volume.astype(jnp.float32) + value_one * sig_one * mask_one).astype(jnp.bfloat16)
    pre_two, patches_two = layer_forward(hidden, kernels[1])
    value_two = pre_two[:, :chans]
    sig_two = jax.nn.sigmoid(pre_two[:, chans:])
    channel_ids = jnp.arange(chans, dtype=jnp.int32)
    weights = 1.0 + 2.0 * (channel_ids[None, :] == canary[:, None]).astype(jnp.float32)
    weights = weights * loss_scale[:, None]
    grad_out = cotangent.astype(jnp.float32) * weights[:, :, None, None, None]
    delta_two = jnp.concatenate(
        [
            grad_out * sig_two * mask_two,
            grad_out * value_two * sig_two * (1.0 - sig_two) * mask_two,
        ],
        axis=1,
    ).astype(jnp.bfloat16)
    grad_two, spread_two = layer_backward(delta_two, kernels[1], patches_two)
    grad_hidden = grad_out + spread_two
    delta_one = jnp.concatenate(
        [
            grad_hidden * sig_one * mask_one,
            grad_hidden * value_one * sig_one * (1.0 - sig_one) * mask_one,
        ],
        axis=1,
    ).astype(jnp.bfloat16)
    grad_one, spread_one = layer_backward(delta_one, kernels[0], patches_one)
    input_grad = grad_hidden + spread_one
    stacked = jnp.stack([grad_one, grad_two], axis=1)
    flat = stacked.reshape((local_ex, -1))
    depth = volume.shape[2] * lax.axis_size("slab")
    bound = 20.0 * jnp.sqrt(jnp.float32(depth * volume.shape[3] * volume.shape[4]))
    examples = local_ex * lax.axis_size("ex")
    scaling = jnp.sqrt(jnp.float32(108 * chans * chans)) / (bound * jnp.sqrt(jnp.float32(examples)))
    summed = lax.psum(flat, "slab")
    norm = jnp.sqrt(jnp.sum(summed * summed, axis=1) + 1e-06)
    factor = jnp.minimum(1.0, bound / norm)
    local_total = jnp.sum(summed * factor[:, None], axis=0)
    total = lax.psum(local_total, "ex")
    kernel_grad = (total * scaling).reshape(kernels.shape)
    return (input_grad, kernel_grad)


def solution(mesh):
    placed = (
        P("ex", None, "slab", None, None),
        P("ex", None, "slab", None, None),
        P("ex", None, "slab", None, None),
        P("ex"),
        P("ex"),
        P(),
    )
    return jax.shard_map(
        per_device,
        mesh=mesh,
        in_specs=placed,
        out_specs=(P("ex", None, "slab", None, None), P()),
        check_vma=False,
    )
```

profile of v0, /device:TPU:1, one launch (start us, length us, event | category | flops | bytes accessed | tf_op | source)
XLA Modules:
  0.0 345.2 jit_solution(6189408591076951782)
XLA Ops:
  7.2 1.3 collective-permute-start.1
  8.5 4.6 %collective-permute-start = (bf16[1,16,1,32,128]{4,3,1,2,0:T(8,128)(2,1)}, bf16[1,16,1,32,128]{4,3,1,2,0:T(8,128)(2,1)S(1)}, u32[]{:S(2)}, u32[]{:S(2)}) collective-permute-start(bf16[1,16,1,32,128]{4,3,1,2,0:T(8,128)(2,1)} %bitcast.510), channel_id=1, source_target_pairs={{0,1},{1,2},{2,3},{3,4},{4,5},{5,6},{6,7},{7,8},{8,9},{9,10},{10,1... | collective-permute-start | bytes 393224 | tf_op jit(solution)/shard_map/ppermute | solution.py:14
  13.1 1.3 convert_bitcast_fusion
  14.4 0.9 collective-permute-done
  15.3 1.6 select_maximum_fusion.5
  19.8 1.4 copy.24
  21.2 0.7 convolution_bitcast_fusion
  22.0 0.8 copy-done.4
  22.8 0.8 add_convert_fusion
  23.5 1.3 collective-permute-start.3
  24.8 5.0 %collective-permute-start.2 = (bf16[1,16,1,32,128]{4,1,3,2,0:T(8,128)(2,1)}, bf16[1,16,1,32,128]{4,1,3,2,0:T(8,128)(2,1)}, u32[]{:S(2)}, u32[]{:S(2)}) collective-permute-start(bf16[1,16,1,32,128]{4,1,3,2,0:T(8,128)(2,1)} %add_convert_fusion), channel_id=1, source_target_pairs={{0,1},{1,2},{2,3},{3,4},{4,5},{5,6},{6,7},{7,8},{8,9},{9,10},{10,1... | collective-permute-start | bytes 393224 | tf_op jit(solution)/shard_map/ppermute | solution.py:14
  29.8 0.6 fusion.118
  31.7 1.5 copy.27
  33.2 1.4 select_maximum_fusion.7
  35.0 0.9 constant_dynamic-update-slice_fusion.49
  36.7 0.9 constant_dynamic-update-slice_fusion.40
  38.4 0.9 constant_dynamic-update-slice_fusion.31
  39.7 0.9 copy.25
  40.7 1.2 fusion.22
  41.9 0.2 multiply_convert_fusion.2
  42.1 1.3 collective-permute-start.5
  43.4 4.2 %collective-permute-start.4 = (bf16[1,32,1,32,128]{4,1,3,2,0:T(8,128)(2,1)S(1)}, bf16[1,32,1,32,128]{4,1,3,2,0:T(8,128)(2,1)S(1)}, u32[]{:S(2)}, u32[]{:S(2)}) collective-permute-start(bf16[1,32,1,32,128]{4,1,3,2,0:T(8,128)(2,1)S(1)} %pad_maximum_fusion), channel_id=1, source_target_pairs={{0,1},{1,2},{2,3},{3,4},{4,5},{5,6},{6,7},{7,8},{8,9},{9,10},{10,1... | collective-permute-start | bytes 786440 | tf_op jit(solution)/shard_map/ppermute | solution.py:14
  47.6 1.2 fusion.37
  48.9 0.4 collective-permute-done.5
  49.3 1.5 collective-permute-done.4
  50.7 2.3 select_maximum_fusion.3
  53.2 0.2 fusion.92
  53.4 0.2 fusion.90
  53.7 0.2 fusion.88
  53.9 0.2 fusion.87
  54.2 0.2 fusion.85
  54.4 0.2 fusion.84
  54.6 0.2 fusion.82
  54.9 0.2 fusion.80
  55.1 0.2 fusion.79
  55.4 0.2 fusion.77
  55.6 0.2 fusion.76
  55.8 0.2 fusion.74
  56.1 0.2 fusion.72
  56.3 0.2 fusion.71
  56.6 1.9 multiply_convert_fusion.1
  58.5 1.1 convolution_bitcast_fusion.1
  59.7 0.9 reshape.189
  60.6 0.9 copy.29
  61.5 230.7 %all-reduce.7.cloned.1.call-done = f32[1,27648]{1,0:T(1,128)} async-done(((f32[1,27648]{1,0:T(1,128)}), f32[1,27648]{1,0:T(1,128)}) %all-reduce.7.cloned.1.call-update) | async-done | bytes 110608 | tf_op jit(solution)/shard_map/psum | solution.py:105
  292.2 1.7 multiply_reduce_fusion
  294.7 1.6 broadcast_multiply_fusion.1
  296.3 1.0 pad_maximum_fusion.1
  297.3 1.3 collective-permute-start.7
  298.6 4.2 %collective-permute-start.6 = (bf16[1,32,1,32,128]{4,1,3,2,0:T(8,128)(2,1)S(1)}, bf16[1,32,1,32,128]{4,1,3,2,0:T(8,128)(2,1)S(1)}, u32[]{:S(2)}, u32[]{:S(2)}) collective-permute-start(bf16[1,32,1,32,128]{4,1,3,2,0:T(8,128)(2,1)S(1)} %pad_maximum_fusion.1), channel_id=1, source_target_pairs={{0,1},{1,2},{2,3},{3,4},{4,5},{5,6},{6,7},{7,8},{8,9},{9,10},{10,1... | collective-permute-start | bytes 786440 | tf_op jit(solution)/shard_map/ppermute | solution.py:14
  302.8 25.1 %all-reduce.9.cloned.1.call-done = f32[27648]{0:T(1024)} async-done(((f32[27648]{0:T(1024)}), f32[27648]{0:T(1024)}) %all-reduce.9.cloned.1.call-update) | async-done | bytes 110608 | tf_op jit(solution)/shard_map/psum | solution.py:109
  327.9 0.9 broadcast_multiply_fusion
  328.8 0.8 reshape.190
  329.6 3.2 select_maximum_fusion
  333.0 0.2 fusion.68
  333.2 0.2 fusion.66
  333.5 0.2 fusion.64
  333.7 0.2 fusion.63
  334.0 0.2 fusion.61
  334.1 0.2 fusion.60
  334.4 0.2 fusion.58
  334.7 0.2 fusion.56
  336.3 1.2 fusion.31
  337.6 0.8 copy.32
  (122 shorter events, 7.9 us)
Async XLA Ops:
  7.2 11.1 %copy-start.6 = (bf16[1,16,1,32,128]{4,3,2,1,0:T(8,128)(2,1)S(1)}, bf16[1,16,1,32,128]{4,3,2,1,0:T(8,128)(2,1)}, u32[]{:S(2)}) copy-start(bf16[1,16,1,32,128]{4,3,2,1,0:T(8,128)(2,1)} %param.6) | copy-start | bytes 393220
  7.2 285.1 %all-reduce.7.cloned.1.call-start = ((), (), s32[]{:S(2)}) async-start(), calls=%async_computation | async-start | bytes 221184 | tf_op jit(solution)/shard_map/psum | solution.py:105
  7.2 8.1 %collective-permute-start.1 = (bf16[1,16,1,32,128]{4,3,2,1,0:T(8,128)(2,1)}, bf16[1,16,1,32,128]{4,3,2,1,0:T(8,128)(2,1)S(1)}, u32[]{:S(2)}, u32[]{:S(2)}) collective-permute-start(bf16[1,16,1,32,128]{4,3,2,1,0:T(8,128)(2,1)} %param.6), channel_id=1, source_target_pairs={{1,0},{2,1},{3,2},{4,3},{5,4},{6,5},{7,6},{8,7},{9,8},{10,9},{11,1... | collective-permute-start | bytes 393224 | tf_op jit(solution)/shard_map/ppermute | solution.py:15
  8.5 6.8 %collective-permute-start = (bf16[1,16,1,32,128]{4,3,1,2,0:T(8,128)(2,1)}, bf16[1,16,1,32,128]{4,3,1,2,0:T(8,128)(2,1)S(1)}, u32[]{:S(2)}, u32[]{:S(2)}) collective-permute-start(bf16[1,16,1,32,128]{4,3,1,2,0:T(8,128)(2,1)} %bitcast.510), channel_id=1, source_target_pairs={{0,1},{1,2},{2,3},{3,4},{4,5},{5,6},{6,7},{7,8},{8,9},{9,10},{10,1... | collective-permute-start | bytes 393224 | tf_op jit(solution)/shard_map/ppermute | solution.py:14
  19.8 1.4 copy-start.11
  21.2 1.6 copy-start.7
  22.0 0.8 copy-start.4
  23.5 9.7 %collective-permute-start.3 = (bf16[1,16,1,32,128]{4,1,3,2,0:T(8,128)(2,1)}, bf16[1,16,1,32,128]{4,1,3,2,0:T(8,128)(2,1)}, u32[]{:S(2)}, u32[]{:S(2)}) collective-permute-start(bf16[1,16,1,32,128]{4,1,3,2,0:T(8,128)(2,1)} %add_convert_fusion), channel_id=1, source_target_pairs={{1,0},{2,1},{3,2},{4,3},{5,4},{6,5},{7,6},{8,7},{9,8},{10,9},{11,1... | collective-permute-start | bytes 393224 | tf_op jit(solution)/shard_map/ppermute | solution.py:15
  24.8 8.4 %collective-permute-start.2 = (bf16[1,16,1,32,128]{4,1,3,2,0:T(8,128)(2,1)}, bf16[1,16,1,32,128]{4,1,3,2,0:T(8,128)(2,1)}, u32[]{:S(2)}, u32[]{:S(2)}) collective-permute-start(bf16[1,16,1,32,128]{4,1,3,2,0:T(8,128)(2,1)} %add_convert_fusion), channel_id=1, source_target_pairs={{0,1},{1,2},{2,3},{3,4},{4,5},{5,6},{6,7},{7,8},{8,9},{9,10},{10,1... | collective-permute-start | bytes 393224 | tf_op jit(solution)/shard_map/ppermute | solution.py:14
  39.7 1.0 copy-start.12
  40.7 1.2 copy-start.9
  40.7 1.2 copy-start.13
  42.1 7.1 %collective-permute-start.5 = (bf16[1,32,1,32,128]{4,1,3,2,0:T(8,128)(2,1)S(1)}, bf16[1,32,1,32,128]{4,1,3,2,0:T(8,128)(2,1)S(1)}, u32[]{:S(2)}, u32[]{:S(2)}) collective-permute-start(bf16[1,32,1,32,128]{4,1,3,2,0:T(8,128)(2,1)S(1)} %pad_maximum_fusion), channel_id=1, source_target_pairs={{1,0},{2,1},{3,2},{4,3},{5,4},{6,5},{7,6},{8,7},{9,8},{10,9},{11,1... | collective-permute-start | bytes 786440 | tf_op jit(solution)/shard_map/ppermute | solution.py:15
  43.4 7.3 %collective-permute-start.4 = (bf16[1,32,1,32,128]{4,1,3,2,0:T(8,128)(2,1)S(1)}, bf16[1,32,1,32,128]{4,1,3,2,0:T(8,128)(2,1)S(1)}, u32[]{:S(2)}, u32[]{:S(2)}) collective-permute-start(bf16[1,32,1,32,128]{4,1,3,2,0:T(8,128)(2,1)S(1)} %pad_maximum_fusion), channel_id=1, source_target_pairs={{0,1},{1,2},{2,3},{3,4},{4,5},{5,6},{6,7},{7,8},{8,9},{9,10},{10,1... | collective-permute-start | bytes 786440 | tf_op jit(solution)/shard_map/ppermute | solution.py:14
  54.9 1.7 copy-start.5
  54.9 1.7 copy-start.10
  58.5 1.1 copy-start
  58.5 1.1 copy-start.2
  60.6 267.4 %all-reduce.9.cloned.1.call-start = ((), (), s32[]{:S(2)}) async-start(), calls=%async_computation.1 | async-start | bytes 221184 | tf_op jit(solution)/shard_map/psum | solution.py:109
  297.3 32.3 %collective-permute-start.7 = (bf16[1,32,1,32,128]{4,1,3,2,0:T(8,128)(2,1)S(1)}, bf16[1,32,1,32,128]{4,1,3,2,0:T(8,128)(2,1)S(1)}, u32[]{:S(2)}, u32[]{:S(2)}) collective-permute-start(bf16[1,32,1,32,128]{4,1,3,2,0:T(8,128)(2,1)S(1)} %pad_maximum_fusion.1), channel_id=1, source_target_pairs={{1,0},{2,1},{3,2},{4,3},{5,4},{6,5},{7,6},{8,7},{9,8},{10,9},{11,1... | collective-permute-start | bytes 786440 | tf_op jit(solution)/shard_map/ppermute | solution.py:15
  298.6 31.1 %collective-permute-start.6 = (bf16[1,32,1,32,128]{4,1,3,2,0:T(8,128)(2,1)S(1)}, bf16[1,32,1,32,128]{4,1,3,2,0:T(8,128)(2,1)S(1)}, u32[]{:S(2)}, u32[]{:S(2)}) collective-permute-start(bf16[1,32,1,32,128]{4,1,3,2,0:T(8,128)(2,1)S(1)} %pad_maximum_fusion.1), channel_id=1, source_target_pairs={{0,1},{1,2},{2,3},{3,4},{4,5},{5,6},{6,7},{7,8},{8,9},{9,10},{10,1... | collective-permute-start | bytes 786440 | tf_op jit(solution)/shard_map/ppermute | solution.py:14
  332.8 1.8 copy-start.1
  332.8 1.8 copy-start.3
  334.6 1.7 copy-start.8
Sparse Core Ops, SparseCore 0:
  60.7 231.5 all-reduce.6
  296.4 31.4 all-reduce.8
where the time goes:
time: 346 us; the launch traced here: 345 us
  waiting for transfers between devices  259 us (75%)
  starting transfers between devices  23.2 us (7%)
  local copies, waits for them, and re-layouts  22.9 us (7%)
  between operations  16.9 us (5%)
  other arithmetic  16.1 us (5%)
  matrix products  7.43 us (2%)
    psum x1, waiting for transfers between devices, per_device(): summed = lax.psum(flat, 'slab')  231 us
    psum x1, waiting for transfers between devices, per_device(): total = lax.psum(local_total, 'ex')  25.1 us
    ppermute x4, starting transfers between devices, with_halo(): before = lax.ppermute(last, axis, up)  17.9 us
    unnamed x131, local copies, waits for them, and re-layouts  15.5 us
    concatenate x4, other arithmetic, with_halo(): array = jnp.concatenate([before, array, after], axis=dim)  8.49 us
  transfers between devices with their start and end apart: 10, of which 5 were waited for; matrix products, arithmetic and copies ran while one was open for 2% of the time, Pallas kernels for 0%

commit v1 on v0

--- a/solution.py
+++ b/solution.py
@@ -102,7 +102,7 @@
     bound = 20.0 * jnp.sqrt(jnp.float32(depth * volume.shape[3] * volume.shape[4]))
     examples = local_ex * lax.axis_size("ex")
     scaling = jnp.sqrt(jnp.float32(108 * chans * chans)) / (bound * jnp.sqrt(jnp.float32(examples)))
-    summed = lax.psum(flat, "slab")
+    summed = jnp.sum(lax.all_gather(flat, "slab"), axis=0)
     norm = jnp.sqrt(jnp.sum(summed * summed, axis=1) + 1e-06)
     factor = jnp.minimum(1.0, bound / norm)
     local_total = jnp.sum(summed * factor[:, None], axis=0)

time: 346 us -> 272 us (0.79)
  waiting for transfers between devices: 259 us -> 154 us
  local copies, waits for them, and re-layouts: 22.9 us -> 40.4 us
  other arithmetic: 16.1 us -> 25.4 us
    psum x1 -> x0, waiting for transfers between devices: 231 us -> none  [per_device(): summed = lax.psum(flat, 'slab')]
    all_gather x0 -> x1, waiting for transfers between devices: none -> 127 us  [per_device(): summed = jnp.sum(lax.all_gather(flat, 'slab'), axis=0)]
    unnamed x131, local copies, waits for them, and re-layouts: 15.5 us -> 32.3 us
    reduce_sum x0 -> x1, other arithmetic: none -> 10.7 us  [per_device(): summed = jnp.sum(lax.all_gather(flat, 'slab'), axis=0)]
  transfers between devices with their start and end apart: 10 -> 10, of which waited for: 5 -> 7; matrix products, arithmetic and copies ran while one was open for 2% -> 13% of each run, Pallas kernels for 0% -> 0%
where the time goes in v1:
time: 272 us; the launch traced here: 271 us
  waiting for transfers between devices  154 us (57%)
  local copies, waits for them, and re-layouts  40.4 us (15%)
  other arithmetic  25.4 us (9%)
  starting transfers between devices  23.9 us (9%)
  between operations  16.7 us (6%)
  matrix products  10.4 us (4%)
    all_gather x1, waiting for transfers between devices, per_device(): summed = jnp.sum(lax.all_gather(flat, 'slab'), axis=0)  127 us
    unnamed x131, local copies, waits for them, and re-layouts  32.3 us
    psum x1, waiting for transfers between devices, per_device(): total = lax.psum(local_total, 'ex')  22.3 us
    ppermute x4, starting transfers between devices, with_halo(): before = lax.ppermute(last, axis, up)  18.7 us
    reduce_sum x1, other arithmetic, per_device(): summed = jnp.sum(lax.all_gather(flat, 'slab'), axis=0)  10.7 us
    concatenate x4, other arithmetic, with_halo(): array = jnp.concatenate([before, array, after], axis=dim)  8.48 us
    dot_general x2, matrix products, layer_backward(): jnp.einsum('otc,etozhw->eczhw', shaped, back_columns(extended), preferred...  6.18 us
  transfers between devices with their start and end apart: 10, of which 7 were waited for; matrix products, arithmetic and copies ran while one was open for 13% of the time, Pallas kernels for 0%

profile of v1, /device:TPU:1, one launch (start us, length us, event | category | flops | bytes accessed | tf_op | source)
XLA Modules:
  0.0 271.3 jit_solution(11392163191259742988)
XLA Ops:
  7.2 1.3 collective-permute-start.1
  8.5 4.6 %collective-permute-start = (bf16[1,16,1,32,128]{4,3,1,2,0:T(8,128)(2,1)}, bf16[1,16,1,32,128]{4,3,1,2,0:T(8,128)(2,1)S(1)}, u32[]{:S(2)}, u32[]{:S(2)}) collective-permute-start(bf16[1,16,1,32,128]{4,3,1,2,0:T(8,128)(2,1)} %bitcast.509), channel_id=1, source_target_pairs={{0,1},{1,2},{2,3},{3,4},{4,5},{5,6},{6,7},{7,8},{8,9},{9,10},{10,1... | collective-permute-start | bytes 393224 | tf_op jit(solution)/shard_map/ppermute | solution.py:14
  13.1 1.3 convert_bitcast_fusion
  14.4 0.9 collective-permute-done
  15.3 1.6 select_maximum_fusion.5
  19.8 1.4 copy.38
  21.2 0.7 convolution_bitcast_fusion
  22.0 0.8 copy-done.4
  22.8 0.8 add_convert_fusion
  23.5 1.3 collective-permute-start.3
  24.8 5.0 %collective-permute-start.2 = (bf16[1,16,1,32,128]{4,1,3,2,0:T(8,128)(2,1)}, bf16[1,16,1,32,128]{4,1,3,2,0:T(8,128)(2,1)}, u32[]{:S(2)}, u32[]{:S(2)}) collective-permute-start(bf16[1,16,1,32,128]{4,1,3,2,0:T(8,128)(2,1)} %add_convert_fusion), channel_id=1, source_target_pairs={{0,1},{1,2},{2,3},{3,4},{4,5},{5,6},{6,7},{7,8},{8,9},{9,10},{10,1... | collective-permute-start | bytes 393224 | tf_op jit(solution)/shard_map/ppermute | solution.py:14
  31.7 1.5 copy.41
  33.2 1.4 select_maximum_fusion.7
  35.0 0.9 constant_dynamic-update-slice_fusion.49
  36.7 0.9 constant_dynamic-update-slice_fusion.40
  38.4 0.9 constant_dynamic-update-slice_fusion.31
  39.7 0.9 copy.39
  40.7 1.2 fusion.22
  42.1 1.3 collective-permute-start.5
  43.4 4.2 %collective-permute-start.4 = (bf16[1,32,1,32,128]{4,1,3,2,0:T(8,128)(2,1)S(1)}, bf16[1,32,1,32,128]{4,1,3,2,0:T(8,128)(2,1)S(1)}, u32[]{:S(2)}, u32[]{:S(2)}) collective-permute-start(bf16[1,32,1,32,128]{4,1,3,2,0:T(8,128)(2,1)S(1)} %pad_maximum_fusion), channel_id=1, source_target_pairs={{0,1},{1,2},{2,3},{3,4},{4,5},{5,6},{6,7},{7,8},{8,9},{9,10},{10,1... | collective-permute-start | bytes 786440 | tf_op jit(solution)/shard_map/ppermute | solution.py:14
  47.6 1.2 fusion.37
  49.3 1.5 collective-permute-done.4
  50.7 2.3 select_maximum_fusion.3
  56.6 1.9 multiply_convert_fusion.1
  58.5 1.1 convolution_bitcast_fusion.1
  59.7 0.9 all_gather_reshape.3
  60.6 1.0 pad_maximum_fusion.1
  61.6 1.3 collective-permute-start.7
  62.9 5.0 %collective-permute-start.6 = (bf16[1,32,1,32,128]{4,1,3,2,0:T(8,128)(2,1)S(1)}, bf16[1,32,1,32,128]{4,1,3,2,0:T(8,128)(2,1)S(1)}, u32[]{:S(2)}, u32[]{:S(2)}) collective-permute-start(bf16[1,32,1,32,128]{4,1,3,2,0:T(8,128)(2,1)S(1)} %pad_maximum_fusion.1), channel_id=1, source_target_pairs={{0,1},{1,2},{2,3},{3,4},{4,5},{5,6},{6,7},{7,8},{8,9},{9,10},{10,1... | collective-permute-start | bytes 786440 | tf_op jit(solution)/shard_map/ppermute | solution.py:14
  67.9 0.9 copy.42
  69.5 1.5 collective-permute-done.6
  71.0 3.2 %select_maximum_fusion = bf16[1,32,3,34,130]{4,1,3,2,0:T(8,128)(2,1)S(1)} fusion(bf16[1,32,1,32,128]{4,1,3,2,0:T(8,128)(2,1)S(1)} %collective-permute-done.7, bf16[1,32,1,32,128]{4,1,3,2,0:T(8,128)(2,1)S(1)} %collective-permute-done.6, bf16[1,16,1,32,128]{4,1,3,2,0:T(8,128)(2,1)} %copy-done.2, bf16[1,16,1,32,128]{4,1,3,2,0:T(8,128)(2,1)} %copy-done), kind=kLoop, calls=%fused_computation.26 | loop fusion | flops 9759360 | bytes 1635072 | tf_op jit(solution)/shard_map/concatenate | solution.py:16
  74.1 0.8 fusion.69
  75.0 0.9 fusion.68
  75.8 0.7 fusion.67
  76.6 0.8 fusion.66
  77.4 0.7 bitcast_dynamic-update-slice_fusion.1
  78.1 0.8 fusion.65
  78.9 0.8 fusion.64
  79.7 0.8 fusion.63
  80.5 0.8 fusion.62
  81.3 0.8 fusion.61
  82.1 0.8 fusion.60
  83.0 0.7 fusion.59
  83.7 0.8 fusion.58
  85.3 0.7 fusion.57
  86.0 0.8 fusion.56
  86.9 0.8 fusion.55
  87.7 0.7 fusion.54
  88.4 0.8 fusion.53
  89.3 0.8 fusion.52
  90.1 0.8 fusion.51
  90.9 0.8 fusion.50
  92.4 0.7 fusion.49
  93.2 0.8 fusion.48
  94.0 0.8 fusion.47
  94.9 0.8 fusion.46
  95.6 127.1 %all-gather.2.cloned.1.call-done = f32[128,1,27648]{2,1,0:T(1,128)} async-done(((f32[1,1,27648]{2,1,0:T(1,128)}), f32[128,1,27648]{2,1,0:T(1,128)}) %all-gather.2.cloned.1.call-update) | async-done | bytes 14155792 | tf_op jit(solution)/shard_map/all_gather | solution.py:105
  222.8 10.7 %reduce_sum.16 = f32[27648]{0:T(1024)S(1)} reduce(f32[128,1,27648]{2,1,0:T(1,128)} %all-gather.2.cloned.1.call-done, f32[]{:T(128)} %constant.8.clone.1), dimensions={0,1}, to_apply=%region_0.1 | reduce | flops 3511296 | bytes 14266372 | tf_op jit(solution)/shard_map/reduce_sum | solution.py:105
  235.4 4.2 %fusion.31 = f32[1,16,1,32,128]{4,1,3,2,0:T(8,128)S(1)} fusion(f32[1,16,1,32,128]{4,1,3,2,0:T(8,128)S(1)} %copy-done.8, bf16[32,27,16,1]{0,2,3,1:T(8,128)(2,1)S(1)} %bitcast.513, bf16[1,27,32,1,32,128]{5,2,4,3,1,0:T(8,128)(2,1)} %fusion.46), kind=kOutput, calls=%fused_computation.43 | convolution fusion | flops 113311744 | bytes 7629824 | tf_op jit(solution)/shard_map/otc,etozhw->eczhw/dot_general | solution.py:59
  239.7 0.8 copy.44
  240.5 22.3 %all-reduce.6.cloned.1.call-done = f32[27648]{0:T(1024)} async-done(((f32[27648]{0:T(1024)}), f32[27648]{0:T(1024)}) %all-reduce.6.cloned.1.call-update) | async-done | bytes 110608 | tf_op jit(solution)/shard_map/psum | solution.py:109
  262.8 0.9 broadcast_multiply_fusion
  263.7 0.8 reshape.195
  (123 shorter events, 13.1 us)
Async XLA Ops:
  7.2 11.1 %copy-start.6 = (bf16[1,16,1,32,128]{4,3,2,1,0:T(8,128)(2,1)S(1)}, bf16[1,16,1,32,128]{4,3,2,1,0:T(8,128)(2,1)}, u32[]{:S(2)}) copy-start(bf16[1,16,1,32,128]{4,3,2,1,0:T(8,128)(2,1)} %param.6) | copy-start | bytes 393220
  7.2 215.6 %all-gather.2.cloned.1.call-start = ((), (), s32[]{:S(2)}) async-start(), calls=%async_computation | async-start | bytes 14266368 | tf_op jit(solution)/shard_map/all_gather | solution.py:105
  7.2 8.1 %collective-permute-start.1 = (bf16[1,16,1,32,128]{4,3,2,1,0:T(8,128)(2,1)}, bf16[1,16,1,32,128]{4,3,2,1,0:T(8,128)(2,1)S(1)}, u32[]{:S(2)}, u32[]{:S(2)}) collective-permute-start(bf16[1,16,1,32,128]{4,3,2,1,0:T(8,128)(2,1)} %param.6), channel_id=1, source_target_pairs={{1,0},{2,1},{3,2},{4,3},{5,4},{6,5},{7,6},{8,7},{9,8},{10,9},{11,1... | collective-permute-start | bytes 393224 | tf_op jit(solution)/shard_map/ppermute | solution.py:15
  8.5 6.8 %collective-permute-start = (bf16[1,16,1,32,128]{4,3,1,2,0:T(8,128)(2,1)}, bf16[1,16,1,32,128]{4,3,1,2,0:T(8,128)(2,1)S(1)}, u32[]{:S(2)}, u32[]{:S(2)}) collective-permute-start(bf16[1,16,1,32,128]{4,3,1,2,0:T(8,128)(2,1)} %bitcast.509), channel_id=1, source_target_pairs={{0,1},{1,2},{2,3},{3,4},{4,5},{5,6},{6,7},{7,8},{8,9},{9,10},{10,1... | collective-permute-start | bytes 393224 | tf_op jit(solution)/shard_map/ppermute | solution.py:14
  19.8 1.4 copy-start.11
  21.2 1.6 copy-start.7
  22.0 0.8 copy-start.4
  23.5 9.7 %collective-permute-start.3 = (bf16[1,16,1,32,128]{4,1,3,2,0:T(8,128)(2,1)}, bf16[1,16,1,32,128]{4,1,3,2,0:T(8,128)(2,1)}, u32[]{:S(2)}, u32[]{:S(2)}) collective-permute-start(bf16[1,16,1,32,128]{4,1,3,2,0:T(8,128)(2,1)} %add_convert_fusion), channel_id=1, source_target_pairs={{1,0},{2,1},{3,2},{4,3},{5,4},{6,5},{7,6},{8,7},{9,8},{10,9},{11,1... | collective-permute-start | bytes 393224 | tf_op jit(solution)/shard_map/ppermute | solution.py:15
  24.8 8.4 %collective-permute-start.2 = (bf16[1,16,1,32,128]{4,1,3,2,0:T(8,128)(2,1)}, bf16[1,16,1,32,128]{4,1,3,2,0:T(8,128)(2,1)}, u32[]{:S(2)}, u32[]{:S(2)}) collective-permute-start(bf16[1,16,1,32,128]{4,1,3,2,0:T(8,128)(2,1)} %add_convert_fusion), channel_id=1, source_target_pairs={{0,1},{1,2},{2,3},{3,4},{4,5},{5,6},{6,7},{7,8},{8,9},{9,10},{10,1... | collective-permute-start | bytes 393224 | tf_op jit(solution)/shard_map/ppermute | solution.py:14
  39.7 1.0 copy-start.12
  40.7 1.2 copy-start.9
  40.7 1.2 copy-start.13
  42.1 7.1 %collective-permute-start.5 = (bf16[1,32,1,32,128]{4,1,3,2,0:T(8,128)(2,1)S(1)}, bf16[1,32,1,32,128]{4,1,3,2,0:T(8,128)(2,1)S(1)}, u32[]{:S(2)}, u32[]{:S(2)}) collective-permute-start(bf16[1,32,1,32,128]{4,1,3,2,0:T(8,128)(2,1)S(1)} %pad_maximum_fusion), channel_id=1, source_target_pairs={{1,0},{2,1},{3,2},{4,3},{5,4},{6,5},{7,6},{8,7},{9,8},{10,9},{11,1... | collective-permute-start | bytes 786440 | tf_op jit(solution)/shard_map/ppermute | solution.py:15
  43.4 7.3 %collective-permute-start.4 = (bf16[1,32,1,32,128]{4,1,3,2,0:T(8,128)(2,1)S(1)}, bf16[1,32,1,32,128]{4,1,3,2,0:T(8,128)(2,1)S(1)}, u32[]{:S(2)}, u32[]{:S(2)}) collective-permute-start(bf16[1,32,1,32,128]{4,1,3,2,0:T(8,128)(2,1)S(1)} %pad_maximum_fusion), channel_id=1, source_target_pairs={{0,1},{1,2},{2,3},{3,4},{4,5},{5,6},{6,7},{7,8},{8,9},{9,10},{10,1... | collective-permute-start | bytes 786440 | tf_op jit(solution)/shard_map/ppermute | solution.py:14
  54.9 1.7 copy-start.5
  54.9 1.7 copy-start.10
  58.5 1.1 copy-start
  58.5 1.1 copy-start.2
  60.6 202.2 %all-reduce.6.cloned.1.call-start = ((), (), s32[]{:S(2)}) async-start(), calls=%async_computation.1 | async-start | bytes 221184 | tf_op jit(solution)/shard_map/psum | solution.py:109
  61.6 7.9 %collective-permute-start.7 = (bf16[1,32,1,32,128]{4,1,3,2,0:T(8,128)(2,1)S(1)}, bf16[1,32,1,32,128]{4,1,3,2,0:T(8,128)(2,1)S(1)}, u32[]{:S(2)}, u32[]{:S(2)}) collective-permute-start(bf16[1,32,1,32,128]{4,1,3,2,0:T(8,128)(2,1)S(1)} %pad_maximum_fusion.1), channel_id=1, source_target_pairs={{1,0},{2,1},{3,2},{4,3},{5,4},{6,5},{7,6},{8,7},{9,8},{10,9},{11,1... | collective-permute-start | bytes 786440 | tf_op jit(solution)/shard_map/ppermute | solution.py:15
  62.9 8.0 %collective-permute-start.6 = (bf16[1,32,1,32,128]{4,1,3,2,0:T(8,128)(2,1)S(1)}, bf16[1,32,1,32,128]{4,1,3,2,0:T(8,128)(2,1)S(1)}, u32[]{:S(2)}, u32[]{:S(2)}) collective-permute-start(bf16[1,32,1,32,128]{4,1,3,2,0:T(8,128)(2,1)S(1)} %pad_maximum_fusion.1), channel_id=1, source_target_pairs={{0,1},{1,2},{2,3},{3,4},{4,5},{5,6},{6,7},{7,8},{8,9},{9,10},{10,1... | collective-permute-start | bytes 786440 | tf_op jit(solution)/shard_map/ppermute | solution.py:14
  74.1 10.5 %copy-start.1 = (bf16[1,16,1,32,128]{4,1,3,2,0:T(8,128)(2,1)S(1)}, bf16[1,16,1,32,128]{4,1,3,2,0:T(8,128)(2,1)}, u32[]{:S(2)}) copy-start(bf16[1,16,1,32,128]{4,1,3,2,0:T(8,128)(2,1)} %copy-done) | copy-start | bytes 393220
  74.1 10.4 %copy-start.3 = (bf16[1,16,1,32,128]{4,1,3,2,0:T(8,128)(2,1)S(1)}, bf16[1,16,1,32,128]{4,1,3,2,0:T(8,128)(2,1)}, u32[]{:S(2)}) copy-start(bf16[1,16,1,32,128]{4,1,3,2,0:T(8,128)(2,1)} %copy-done.2) | copy-start | bytes 393220
  95.6 139.8 %copy-start.8 = (f32[1,16,1,32,128]{4,1,3,2,0:T(8,128)S(1)}, f32[1,16,1,32,128]{4,1,3,2,0:T(8,128)}, u32[]{:S(2)}) copy-start(f32[1,16,1,32,128]{4,1,3,2,0:T(8,128)} %get-tuple-element.16) | copy-start | bytes 786436
Sparse Core Ops, SparseCore 0:
  60.7 162.0 all-gather.1
  235.6 27.1 all-reduce.5
